TPU v7x, 512 devices: a whole 4x4x16 slice. The times are simulated.
512 devices in a mesh: dom: 64 (over z, y), src: 4 (over x), rel: 2 (over core).
Axes of the slice: x: 4, y: 4, z: 16, core: 2. Of those that a mesh axis runs over, the one named last changes fastest.
Arguments:
- source_feats: bfloat16 [131072, 256], P(('dom', 'src', 'rel')), may hold values from -6 to 6
- rel_weight: bfloat16 [12, 256, 256], P('rel'), may hold values from -0.375 to 0.375
- halo_pick: int32 [64, 4, 2, 64], P('dom', 'src', 'rel'), may hold values from 0 to 1
- entry_index: int32 [64, 4, 2, 3, 64], P('dom', 'src', 'rel'), may hold values from 0 to 63, as said below
- entry_count: int32 [64, 4, 2], P('dom', 'src', 'rel'), may hold values from 1 to 64, as said below
- entry_values: bfloat16 [64, 4, 2, 64, 128, 128], P('dom', 'src', 'rel'), may hold values from -0.125 to 0.125
- cotangent: bfloat16 [131072, 256], P(('dom', 'src', 'rel')), may hold values from -0.0546875 to 0.0546875
Outputs:
- out_feats: bfloat16 [131072, 256], P(('dom', 'src', 'rel'))
- grad_rel: float32 [12, 256, 256], P('rel')
Inputs may be any that keep to these rules, and one draw needn't show every extreme that they name: `entry_index`: row 0 of an entry is a target block below 16, row 1 a partition below 64, row 2 a relation below 6. Over all 64 entries of one (p,s,g), every partition is named 64 // 64 times or once more. `entry_count`: live entries come first; some (p,s,g) has all 64 entries live in every draw.
All inputs are finite; a program needn't handle non-finite values.
Results may differ from a plain program's by a relative error of at most 0.0057.
Values may be sent and summed in bfloat16 or wider, within the bound.
A program may use at most 64 MiB of HBM per device.

v0:
```python
import jax
import jax.numpy as jnp
from jax import lax
from jax.sharding import PartitionSpec as P


def silu_slope(pre_values):
    logistic = jax.nn.sigmoid(pre_values)
    return logistic * (1.0 + pre_values * (1.0 - logistic))


def local(source_feats, rel_weight, halo_pick, entry_index, entry_count, entry_values, cotangent):
    partitions = lax.axis_size("dom")
    tile_rows = entry_values.shape[-1]
    features = source_feats.shape[1]
    chosen = halo_pick.reshape(-1)
    everyone = lax.all_gather(source_feats, "dom", axis=0, tiled=True)
    everyone = everyone.reshape(partitions, -1, tile_rows, features)
    halo_blocks = everyone[jnp.arange(partitions, dtype=jnp.int32), chosen]
    own_rows = cotangent.shape[0]
    tgt_blocks = own_rows * lax.axis_size("src") * lax.axis_size("rel") // tile_rows
    rel_local = rel_weight.shape[0]
    entry_table = entry_index.reshape(3, -1)
    slot_total = entry_table.shape[1]
    values = entry_values.reshape(-1, tile_rows, tile_rows)
    picked = halo_blocks[entry_table[1]]
    messages = jnp.einsum("eij,ejd->eid", values, picked, preferred_element_type=jnp.float32)
    live_mask = jnp.arange(slot_total, dtype=jnp.int32) < entry_count.reshape(())
    target_slot = entry_table[2] * tgt_blocks + entry_table[0]
    slot_numbers = jnp.arange(rel_local * tgt_blocks, dtype=jnp.int32)
    placement = ((slot_numbers[:, None] == target_slot[None, :]) & live_mask[None, :]).astype(
        jnp.float32
    )
    totals = jnp.einsum(
        "se,eid->sid",
        placement,
        messages,
        precision=lax.Precision.HIGHEST,
        preferred_element_type=jnp.float32,
    )
    relation_terms = totals.astype(jnp.bfloat16).reshape(
        rel_local, tgt_blocks * tile_rows, features
    )
    summed = lax.psum_scatter(
        jnp.einsum("rtd,rde->te", relation_terms, rel_weight, preferred_element_type=jnp.float32),
        ("src", "rel"),
        scatter_dimension=0,
        tiled=True,
    )
    out_feats = jax.nn.silu(summed).astype(jnp.bfloat16)
    local_grad = (cotangent.astype(jnp.float32) * silu_slope(summed)).astype(jnp.bfloat16)
    grad_rows = lax.all_gather(local_grad, ("src", "rel"), axis=0, tiled=True)
    weight_terms = jnp.einsum(
        "rtd,te->rde", relation_terms, grad_rows, preferred_element_type=jnp.float32
    )
    grad_rel = lax.psum(weight_terms, ("dom", "src"))
    return (out_feats, grad_rel)


def solution(mesh):
    return jax.shard_map(
        local,
        mesh=mesh,
        in_specs=(
            P(("dom", "src", "rel"), None),
            P("rel", None, None),
            P("dom", "src", "rel", None),
            P("dom", "src", "rel", None, None),
            P("dom", "src", "rel"),
            P("dom", "src", "rel", None, None, None),
            P(("dom", "src", "rel"), None),
        ),
        out_specs=(P(("dom", "src", "rel"), None), P("rel", None, None)),
        check_vma=False,
    )
```

profile of v0, /device:TPU:2, one launch (start us, length us, event | category | flops | bytes accessed | tf_op | source)
XLA Modules:
  0.0 711.4 jit_solution(15321850771566686382)
XLA Ops:
  7.2 0.0 copy-start
  7.2 0.0 all-gather.3.cloned.1.call-start
  7.2 0.7 all-gather.3.cloned.1.call-update
  7.9 0.0 reduce-scatter.2.cloned.1.call-start
  8.6 0.7 fusion.17
  9.3 0.7 add_bitcast_fusion
  10.0 0.7 fusion.18
  10.6 160.9 %all-gather.3.cloned.1.call-done = bf16[16384,256]{1,0:T(8,128)(2,1)} async-done(((bf16[256,256]{1,0:T(8,128)(2,1)}), bf16[16384,256]{1,0:T(8,128)(2,1)}) %all-gather.3.cloned.1.call-update) | async-done | bytes 8388624 | tf_op jit(solution)/shard_map/all_gather | solution.py:17
  171.5 6.2 gather_fusion
  177.7 4.9 gather_fusion.1
  182.6 0.0 copy-done
  182.6 6.7 fusion.5
  189.3 9.2 %copy.12 = f32[64,256,128]{1,0,2:T(8,128)} copy(f32[64,256,128]{2,1,0:T(8,128)} %fusion.5) | data formatting | bytes 16777216 | tf_op jit(solution)/shard_map/eij,ejd->eid/dot_general | solution.py:27
  198.5 8.4 %fusion.2 = bf16[96,128,256]{2,0,1:T(8,128)(2,1)S(1)} fusion(f32[64,256,128]{1,0,2:T(8,128)} %copy.12, s32[64]{0:T(128)S(1)} %add_bitcast_fusion, pred[64]{0:T(512)(128)(4,1)S(1)} %iota_compare_fusion.1), kind=kOutput, calls=%fused_computation.4 | convolution fusion | flops 2419077120 | bytes 14680384 | tf_op jit(solution)/shard_map/se,eid->sid/dot_general | solution.py:34
  207.0 0.0 copy-start.3
  207.0 3.7 copy.10
  210.6 0.0 copy-start.1
  210.6 2.6 copy-done.1
  213.3 0.0 copy-done.3
  213.3 0.0 copy-start.2
  213.3 3.3 convolution_bitcast_fusion
  216.5 0.0 reduce-scatter.2.cloned.1.call-update
  216.6 0.0 all-gather.5.cloned.1.call-start
  216.6 33.4 %reduce-scatter.2.cloned.1.call-done = f32[256,256]{1,0:T(8,128)} async-done(((f32[2048,256]{1,0:T(8,128)}), f32[256,256]{1,0:T(8,128)}) %reduce-scatter.2.cloned.1.call-update) | async-done | bytes 262160 | tf_op jit(solution)/shard_map/reduce_scatter | solution.py:44
  250.0 0.0 copy-done.2
  250.0 1.8 multiply_convert_fusion
  251.7 0.0 all-gather.5.cloned.1.call-update
  251.8 0.0 all-reduce.2.cloned.1.call-start
  251.8 32.6 %all-gather.5.cloned.1.call-done = bf16[2048,256]{1,0:T(8,128)(2,1)} async-done(((bf16[256,256]{1,0:T(8,128)(2,1)}), bf16[2048,256]{1,0:T(8,128)(2,1)}) %all-gather.5.cloned.1.call-update) | async-done | bytes 1048592 | tf_op jit(solution)/shard_map/all_gather | solution.py:52
  284.4 6.0 fusion.7
  290.4 0.0 all-reduce.2.cloned.1.call-update
  290.4 411.6 %all-reduce.2.cloned.1.call-done = f32[6,256,256]{2,1,0:T(8,128)} async-done(((f32[6,256,256]{2,1,0:T(8,128)}), f32[6,256,256]{2,1,0:T(8,128)}) %all-reduce.2.cloned.1.call-update) | async-done | bytes 1572880 | tf_op jit(solution)/shard_map/psum | solution.py:56
  702.1 2.7 copy.16
  (2 shorter events, 0.0 us)
Async XLA Ops:
  7.2 175.5 %copy-start = (bf16[1,1,1,64,128,128]{5,4,3,2,1,0:T(8,128)(2,1)S(1)}, bf16[1,1,1,64,128,128]{5,4,3,2,1,0:T(8,128)(2,1)}, u32[]{:S(2)}) copy-start(bf16[1,1,1,64,128,128]{5,4,3,2,1,0:T(8,128)(2,1)} %param.12) | copy-start | bytes 6291460
  7.2 164.4 %all-gather.3.cloned.1.call-start = ((), (), s32[]{:S(2)}) async-start(), calls=%async_computation.1 | async-start | bytes 8519680 | tf_op jit(solution)/shard_map/all_gather | solution.py:17
  7.9 242.1 %reduce-scatter.2.cloned.1.call-start = ((), (), s32[]{:S(2)}) async-start(), calls=%async_computation.2 | async-start | bytes 2359296 | tf_op jit(solution)/shard_map/reduce_scatter | solution.py:44
  207.0 6.3 copy-start.3
  210.6 2.7 copy-start.1
  213.3 36.7 %copy-start.2 = (bf16[256,256]{1,0:T(8,128)(2,1)S(1)}, bf16[256,256]{1,0:T(8,128)(2,1)}, u32[]{:S(2)}) copy-start(bf16[256,256]{1,0:T(8,128)(2,1)} %param.13) | copy-start | bytes 393220
  216.6 67.8 %all-gather.5.cloned.1.call-start = ((), (), s32[]{:S(2)}) async-start(), calls=%async_computation.3 | async-start | bytes 1179648 | tf_op jit(solution)/shard_map/all_gather | solution.py:52
  251.8 450.3 %all-reduce.2.cloned.1.call-start = ((), (), s32[]{:S(2)}) async-start(), calls=%async_computation.4 | async-start | bytes 3145728 | tf_op jit(solution)/shard_map/psum | solution.py:56
Sparse Core Ops, SparseCore 0:
  10.9 160.5 all-gather.2
  216.7 33.2 reduce-scatter.1
  252.7 31.6 all-gather.4
  290.6 411.4 all-reduce.1
where the time goes:
time: 712 us; the launch traced here: 711 us
  waiting for transfers between devices  639 us (90%)
  local copies, waits for them, and re-layouts  29.3 us (4%)
  matrix products  24.4 us (3%)
  between operations  14.5 us (2%)
    psum x1, waiting for transfers between devices, local(): grad_rel = lax.psum(weight_terms, ('dom', 'src'))  412 us
    all_gather x1, waiting for transfers between devices, local(): everyone = lax.all_gather(source_feats, 'dom', axis=0, tiled=True)  161 us
    reduce_scatter x1, waiting for transfers between devices, local(): lax.psum_scatter(jnp.einsum('rtd,rde->te', relation_terms, rel_weight, pr...  33.4 us
    all_gather x1, waiting for transfers between devices, local(): grad_rows = lax.all_gather(local_grad, ('src', 'rel'), axis=0, tiled=True)  32.6 us
  transfers between devices with their start and end apart: 4, of which 4 were waited for; matrix products, arithmetic and copies ran while one was open for 0% of the time, Pallas kernels for 0%

commit v1 on v0

--- a/solution.py
+++ b/solution.py
@@ -2,6 +2,10 @@
 import jax.numpy as jnp
 from jax import lax
 from jax.sharding import PartitionSpec as P
+
+
+def try_all_sites_now(frame):
+    return jax.lax.psum(jax.lax.psum(frame, axis_name="src"), axis_name="dom")
 
 
 def silu_slope(pre_values):
@@ -53,7 +57,7 @@
     weight_terms = jnp.einsum(
         "rtd,te->rde", relation_terms, grad_rows, preferred_element_type=jnp.float32
     )
-    grad_rel = lax.psum(weight_terms, ("dom", "src"))
+    grad_rel = try_all_sites_now(weight_terms)
     return (out_feats, grad_rel)
 
 

time: 712 us -> 650 us (0.913)
  waiting for transfers between devices: 639 us -> 577 us
    psum x1 -> x2, waiting for transfers between devices: 412 us -> 350 us  [try_all_sites_now(): return jax.lax.psum(jax.lax.psum(frame, axis_name='src'), axis_name='dom')]
  transfers between devices with their start and end apart: 4 -> 5, of which waited for: 4 -> 5; matrix products, arithmetic and copies ran while one was open for 0% -> 0% of each run, Pallas kernels for 0% -> 0%
where the time goes in v1:
time: 650 us
  waiting for transfers between devices  577 us (89%)
  local copies, waits for them, and re-layouts  29.3 us (5%)
  matrix products  24.4 us (4%)
  between operations  14.5 us (2%)
    psum x2, waiting for transfers between devices, try_all_sites_now(): return jax.lax.psum(jax.lax.psum(frame, axis_name='src'), axis_name='dom')  350 us
    all_gather x1, waiting for transfers between devices, local(): everyone = lax.all_gather(source_feats, 'dom', axis=0, tiled=True)  161 us
    reduce_scatter x1, waiting for transfers between devices, local(): lax.psum_scatter(jnp.einsum('rtd,rde->te', relation_terms, rel_weight, pr...  33.4 us
    all_gather x1, waiting for transfers between devices, local(): grad_rows = lax.all_gather(local_grad, ('src', 'rel'), axis=0, tiled=True)  32.6 us
  transfers between devices with their start and end apart: 5, of which 5 were waited for; matrix products, arithmetic and copies ran while one was open for 0% of the time, Pallas kernels for 0%

profile of v1, /device:TPU:2, one launch (start us, length us, event | category | flops | bytes accessed | tf_op | source)
XLA Modules:
  0.0 649.6 jit_solution(5026396538015346244)
XLA Ops:
  7.2 0.0 copy-start
  7.2 0.0 all-gather.3.cloned.1.call-start
  7.2 0.7 all-gather.3.cloned.1.call-update
  7.9 0.0 reduce-scatter.2.cloned.1.call-start
  8.6 0.7 fusion.17
  9.3 0.7 add_bitcast_fusion
  10.0 0.7 fusion.18
  10.6 160.9 %all-gather.3.cloned.1.call-done = bf16[16384,256]{1,0:T(8,128)(2,1)} async-done(((bf16[256,256]{1,0:T(8,128)(2,1)}), bf16[16384,256]{1,0:T(8,128)(2,1)}) %all-gather.3.cloned.1.call-update) | async-done | bytes 8388624 | tf_op jit(solution)/shard_map/all_gather | solution.py:21
  171.5 6.2 gather_fusion
  177.7 4.9 gather_fusion.1
  182.6 0.0 copy-done
  182.6 6.7 %fusion.5 = f32[64,256,128]{2,1,0:T(8,128)} fusion(bf16[64,128,256]{2,1,0:T(8,128)(2,1)} %gather_fusion.1, bf16[1,1,1,64,128,128]{5,4,3,2,1,0:T(8,128)(2,1)S(1)} %copy-done), kind=kOutput, calls=%fused_computation.6 | convolution fusion | flops 536870912 | bytes 14680064 | tf_op jit(solution)/shard_map/eij,ejd->eid/dot_general | solution.py:31
  189.3 9.2 %copy.12 = f32[64,256,128]{1,0,2:T(8,128)} copy(f32[64,256,128]{2,1,0:T(8,128)} %fusion.5) | data formatting | bytes 16777216 | tf_op jit(solution)/shard_map/eij,ejd->eid/dot_general | solution.py:31
  198.5 8.4 %fusion.2 = bf16[96,128,256]{2,0,1:T(8,128)(2,1)S(1)} fusion(f32[64,256,128]{1,0,2:T(8,128)} %copy.12, s32[64]{0:T(128)S(1)} %add_bitcast_fusion, pred[64]{0:T(512)(128)(4,1)S(1)} %iota_compare_fusion.1), kind=kOutput, calls=%fused_computation.4 | convolution fusion | flops 2419077120 | bytes 14680384 | tf_op jit(solution)/shard_map/se,eid->sid/dot_general | solution.py:38
  207.0 0.0 copy-start.3
  207.0 3.7 copy.10
  210.6 0.0 copy-start.1
  210.6 2.6 copy-done.1
  213.3 0.0 copy-done.3
  213.3 0.0 copy-start.2
  213.3 3.3 convolution_bitcast_fusion
  216.5 0.0 reduce-scatter.2.cloned.1.call-update
  216.6 0.0 all-gather.5.cloned.1.call-start
  216.6 33.4 %reduce-scatter.2.cloned.1.call-done = f32[256,256]{1,0:T(8,128)} async-done(((f32[2048,256]{1,0:T(8,128)}), f32[256,256]{1,0:T(8,128)}) %reduce-scatter.2.cloned.1.call-update) | async-done | bytes 262160 | tf_op jit(solution)/shard_map/reduce_scatter | solution.py:48
  250.0 0.0 copy-done.2
  250.0 1.8 multiply_convert_fusion
  251.7 0.0 all-gather.5.cloned.1.call-update
  251.8 0.0 all-reduce.3.cloned.1.call-start
  251.8 32.6 %all-gather.5.cloned.1.call-done = bf16[2048,256]{1,0:T(8,128)(2,1)} async-done(((bf16[256,256]{1,0:T(8,128)(2,1)}), bf16[2048,256]{1,0:T(8,128)(2,1)}) %all-gather.5.cloned.1.call-update) | async-done | bytes 1048592 | tf_op jit(solution)/shard_map/all_gather | solution.py:56
  284.4 6.0 fusion.7
  290.4 0.0 all-reduce.3.cloned.1.call-update
  290.4 0.0 all-reduce.5.cloned.1.call-start
  290.5 66.1 %all-reduce.3.cloned.1.call-done = f32[6,256,256]{2,1,0:T(8,128)} async-done(((f32[6,256,256]{2,1,0:T(8,128)}), f32[6,256,256]{2,1,0:T(8,128)}) %all-reduce.3.cloned.1.call-update) | async-done | bytes 1572880 | tf_op jit(solution)/shard_map/psum | solution.py:8
  356.6 0.0 all-reduce.5.cloned.1.call-update
  356.6 283.7 %all-reduce.5.cloned.1.call-done = f32[6,256,256]{2,1,0:T(8,128)} async-done(((f32[6,256,256]{2,1,0:T(8,128)}), f32[6,256,256]{2,1,0:T(8,128)}) %all-reduce.5.cloned.1.call-update) | async-done | bytes 1572880 | tf_op jit(solution)/shard_map/psum | solution.py:8
  640.3 2.7 copy.17
  (2 shorter events, 0.0 us)
Async XLA Ops:
  7.2 175.5 %copy-start = (bf16[1,1,1,64,128,128]{5,4,3,2,1,0:T(8,128)(2,1)S(1)}, bf16[1,1,1,64,128,128]{5,4,3,2,1,0:T(8,128)(2,1)}, u32[]{:S(2)}) copy-start(bf16[1,1,1,64,128,128]{5,4,3,2,1,0:T(8,128)(2,1)} %param.12) | copy-start | bytes 6291460
  7.2 164.4 %all-gather.3.cloned.1.call-start = ((), (), s32[]{:S(2)}) async-start(), calls=%async_computation.1 | async-start | bytes 8519680 | tf_op jit(solution)/shard_map/all_gather | solution.py:21
  7.9 242.1 %reduce-scatter.2.cloned.1.call-start = ((), (), s32[]{:S(2)}) async-start(), calls=%async_computation.2 | async-start | bytes 2359296 | tf_op jit(solution)/shard_map/reduce_scatter | solution.py:48
  207.0 6.3 copy-start.3
  210.6 2.7 copy-start.1
  213.3 36.7 %copy-start.2 = (bf16[256,256]{1,0:T(8,128)(2,1)S(1)}, bf16[256,256]{1,0:T(8,128)(2,1)}, u32[]{:S(2)}) copy-start(bf16[256,256]{1,0:T(8,128)(2,1)} %param.13) | copy-start | bytes 393220
  216.6 67.8 %all-gather.5.cloned.1.call-start = ((), (), s32[]{:S(2)}) async-start(), calls=%async_computation.3 | async-start | bytes 1179648 | tf_op jit(solution)/shard_map/all_gather | solution.py:56
  251.8 104.8 %all-reduce.3.cloned.1.call-start = ((), (), s32[]{:S(2)}) async-start(), calls=%async_computation.4 | async-start | bytes 3145728 | tf_op jit(solution)/shard_map/psum | solution.py:8
  290.4 349.9 %all-reduce.5.cloned.1.call-start = ((), (), s32[]{:S(2)}) async-start(), calls=%async_computation.5 | async-start | bytes 3145728 | tf_op jit(solution)/shard_map/psum | solution.py:8
Sparse Core Ops, SparseCore 0:
  10.9 160.5 all-gather.2
  216.7 33.2 reduce-scatter.1
  252.7 31.6 all-gather.4
  290.6 65.9 all-reduce.2
  359.9 280.4 all-reduce.4
